TPU v7x, 32 devices: a whole 2x2x4 slice. The times are simulated.
32 devices in a mesh: span: 4 (over z), mp: 4 (over x, core), phase: 2 (over y).
Axes of the slice: x: 2, y: 2, z: 4, core: 2. Of those that a mesh axis runs over, the one named last changes fastest.
Arguments:
- latents: bfloat16 [4096, 2560], P(('span', 'phase')), may hold values from -6 to 6
- w_qkv: bfloat16 [2560, 3, 1536], P(None, None, 'mp'), may hold values from -0.125 to 0.125
- w_out: bfloat16 [1536, 2560], P('mp'), may hold values from -0.15625 to 0.15625
- decay: float32 [4, 2, 12], P('span', None, 'mp'), may hold values from 0.4 to 0.999, as said below
- frame_ids: int32 [4, 1024], P('span'), may hold values from 0 to 15, never falling along the last dimension, each value on 1 to 256 neighbouring positions
- memory_mask: int32 [4, 17], P('span'), may hold values 0 or 1
Outputs:
- refined: bfloat16 [4096, 2560], P(('span', 'phase'), 'mp')
Inputs may be any that keep to these rules, and one draw needn't show every extreme that they name: `frame_ids`: along each span's 1024 tokens the frame numbers never fall, and every frame from 0 on holds 1 to 256 tokens. `decay`: every entry lies strictly between 0 and 1.
All inputs are finite; a program needn't handle non-finite values. No bound on the sum of `memory_mask` on one device may be relied on, other than what follows from the above.
Results may differ from a plain program's by a relative error of at most 0.004.
Values may be sent and summed in bfloat16 or wider, within the bound.
A program may use at most 128 MiB of HBM per device.

v0:
```python
import functools
import math

import jax
import jax.numpy as jnp
from jax import lax
from jax.experimental import pallas as pl
from jax.experimental.pallas import tpu as pltpu
from jax.sharding import PartitionSpec as P

HD = 128
WIN = 64
MEM = 256
HALF = WIN // 2
GROUP = 128
PIECES = 8
EARLY = 2
MESH = pl.DeviceIdType.MESH

outside_frame = 1048576
epsilon = 1e-06
score_factor = HD ** (-0.5) * math.log2(math.e)


def remote(src, dst, send, recv, where):
    return pltpu.make_async_remote_copy(
        src_ref=src, dst_ref=dst, send_sem=send, recv_sem=recv,
        device_id=where, device_id_type=MESH,
    )


def body(
    sizes, x_hbm, w_hbm, wo_hbm, decay, frames, opened, out,
    x, w, wo, kv, q, num, den, att, fr, tail_in, s_in, s_out, m_out, mem,
    load_sem, ws_send, ws_recv, wo_send, wo_recv, wm_send, wm_recv, wr_send, wr_recv, y_send, y_recv, z_send, z_recv, m_send, m_recv,
    h_send, h_recv, a_send, a_recv, c_send, c_recv, r_send, r_recv,
):
    n_span, n_mp, rows, width, cols = sizes
    heads = cols // HD
    share = width // n_mp
    groups = kv.shape[1] // GROUP
    c = lax.axis_index("span")
    me = lax.axis_index("mp")
    phase = lax.axis_index("phase")
    is0 = phase == 0
    other = 1 - phase
    kept, sent = phase, 1 - phase
    sib = me + 1 - 2 * (me % 2)
    chips = n_mp // 2
    tail0 = HALF + rows - MEM
    piece = MEM // PIECES

    def load(i, src, dst):
        copy = pltpu.make_async_copy(src, dst, load_sem.at[i])
        copy.start()
        return copy

    top = rows - MEM
    x_tail = load(0, x_hbm.at[pl.ds(top, MEM)], x.at[pl.ds(top, MEM)])
    w_sent = load(1, w_hbm.at[1 + sent], w.at[:, pl.ds(0, cols)])
    w_kept = load(2, w_hbm.at[1 + kept], w.at[:, pl.ds(cols, cols)])
    x_head = load(3, x_hbm.at[pl.ds(0, top)], x.at[pl.ds(0, top)])
    w_query = load(4, w_hbm.at[0], w.at[:, pl.ds(2 * cols, cols)])
    wo_own = load(5, wo_hbm.at[:, pl.ds(pl.multiple_of(me * share, HD), share)], wo.at[me])

    barrier = pltpu.get_barrier_semaphore()
    for o in range(1, n_mp):
        pl.semaphore_signal(barrier, inc=1, device_id={"mp": (me + o) % n_mp}, device_id_type=MESH)
    pl.semaphore_signal(barrier, inc=1, device_id={"phase": other}, device_id_type=MESH)

    @pl.when(c > 0)
    def _():
        pl.semaphore_signal(barrier, inc=1, device_id={"span": c - 1}, device_id_type=MESH)

    @pl.when(c < n_span - 1)
    def _():
        pl.semaphore_signal(barrier, inc=1, device_id={"span": c + 1}, device_id_type=MESH)

    pl.semaphore_wait(barrier, n_mp + 1 + (c + n_span - 1) // n_span - (c + 1) // n_span)

    part = cols // 3 // HALF * HALF
    middle = cols - 2 * part
    my_part = pl.ds(pl.multiple_of(phase * (part + middle), HALF), part)
    middle_part = pl.ds(part, middle)

    def columns_of(m):
        return pl.ds(pl.multiple_of(m * share, HD), share)

    wo_side = remote(wo_hbm.at[:, columns_of(sib)], wo.at[me], ws_send, ws_recv, {"mp": sib})
    wo_copies, wo_relays, wo_middles = [], [], []
    for o in range(1, chips):
        for i, near in enumerate((me, sib)):
            to, source = (near + 2 * o) % n_mp, (near + n_mp - 2 * o) % n_mp
            at = 2 * (o - 1) + i
            wo_copies.append(remote(
                wo_hbm.at[my_part, columns_of(to)], wo.at[me, my_part],
                wo_send.at[at], wo_recv.at[at], {"mp": to},
            ))
            wo_middles.append(remote(
                wo_hbm.at[middle_part, columns_of(to)], wo.at[me, middle_part],
                wm_send.at[at], wm_recv.at[at], {"mp": to},
            ))
            wo_relays.append(remote(
                wo.at[source, my_part], wo.at[source, my_part],
                wr_send.at[at], wr_recv.at[at], {"phase": other},
            ))
    for copy in wo_copies + wo_middles:
        copy.start()
    wo_side.start()

    def unit(raw, flag):
        parts = []
        for i in range(heads):
            part = raw[:, i * HD:(i + 1) * HD]
            scale = lax.rsqrt(jnp.mean(part * part, axis=-1, keepdims=True) + epsilon)
            if flag is not None:
                scale = jnp.where(flag, scale, 1.0)
            parts.append((part * scale).astype(jnp.bfloat16))
        return jnp.concatenate(parts, axis=1)

    def project(first, count, column):
        return jnp.dot(
            x[first:first + count, :], w[:, column:column + cols],
            preferred_element_type=jnp.float32,
        )

    zero_rows = kv.shape[1] - (HALF + rows + HALF)
    kv[:, HALF + rows + HALF:, :] = jnp.zeros((2, zero_rows, cols), jnp.bfloat16)
    q[HALF + rows:, :] = jnp.zeros((q.shape[0] - HALF - rows, cols), jnp.bfloat16)
    q[:HALF, :] = jnp.zeros((HALF, cols), jnp.bfloat16)
    blank = pl.multiple_of(phase * (HALF + rows), HALF)
    kv[:, pl.ds(blank, HALF), :] = jnp.zeros((2, HALF, cols), jnp.bfloat16)

    @pl.when(c == 0)
    def _():
        s_in[...] = jnp.zeros(s_in.shape, s_in.dtype)

    x_tail.wait()
    w_sent.wait()
    kv[sent, tail0:tail0 + MEM, :] = unit(project(top, MEM, 0), sent == 0)
    tails, chain, moved = [], [], []
    for k in range(PIECES):
        at = pl.ds(k * piece, piece)
        copy = remote(
            kv.at[sent, pl.ds(tail0 + k * piece, piece)], tail_in.at[at],
            y_send.at[k], y_recv.at[k], {"phase": other},
        )
        copy.start()
        tails.append(copy)
        chain.append(remote(s_out.at[at], s_in.at[at], z_send.at[k], z_recv.at[k], {"span": (c + 1) % n_span}))
        moved.append(remote(m_out.at[at], mem.at[kept, at], m_send.at[k], m_recv.at[k], {"phase": other}))
    w_kept.wait()
    kv[kept, tail0:tail0 + MEM, :] = unit(project(top, MEM, cols), kept == 0)
    x_head.wait()
    kv[sent, HALF:HALF + top, :] = unit(project(0, top, 0), sent == 0)
    kv[kept, HALF:HALF + top, :] = unit(project(0, top, cols), kept == 0)
    halo_from = pl.multiple_of(HALF + other * (rows - HALF), HALF)
    halo = remote(
        kv.at[:, pl.ds(halo_from, HALF)], kv.at[:, pl.ds(blank, HALF)],
        h_send, h_recv, {"phase": other},
    )
    halo.start()

    def row_of(half):
        return jnp.concatenate(
            [jnp.broadcast_to(decay[half:half + 1, i:i + 1], (1, HD)) for i in range(heads)], axis=1
        )

    r0, r1 = row_of(0), row_of(1)

    def mix(rate):
        return jnp.where(is0, 1.0 - rate, jnp.sqrt(1.0 - rate * rate))

    f0, f1, both = mix(r0), mix(r1), r0 * r1

    def chain_piece(k):
        at = slice(k * piece, (k + 1) * piece)
        own = kv[kept, tail0 + k * piece:tail0 + (k + 1) * piece, :].astype(jnp.float32)
        tails[k].wait_recv()
        theirs = tail_in[at, :].astype(jnp.float32)
        low = f0 * jnp.where(is0, own, theirs)
        high = r1 * low + f1 * jnp.where(is0, theirs, own)

        @pl.when(c > 0)
        def _():
            chain[k].wait_recv()

        state = s_in[at, :].astype(jnp.float32)
        s_out[at, :] = (both * state + high).astype(jnp.bfloat16)

        @pl.when(c < n_span - 1)
        def _():
            chain[k].start()

        later = r0 * state + low
        m_out[at, :] = jnp.where(is0, later, state).astype(jnp.bfloat16)
        moved[k].start()
        mem[kept, at, :] = jnp.where(is0, state, later).astype(jnp.bfloat16)

    def queries():
        w_query.wait()
        for first in (0, top):
            count = top if first == 0 else rows - top
            q[HALF + first:HALF + first + count, :] = unit(project(first, count, 2 * cols), None)

    def frame_rows():
        total = frames.shape[1]
        wide = jnp.broadcast_to(frames[...], (8, total))
        ahead = pltpu.roll(wide, HALF, 1)
        behind = pltpu.roll(wide, total - (rows - HALF), 1)
        place = lax.broadcasted_iota(jnp.int32, wide.shape, 1)
        ext = jnp.where(is0, ahead, behind)
        least = jnp.where(is0, HALF, 0)
        limit = jnp.where(is0, total + HALF, rows + HALF)
        ext = jnp.where((place >= least) & (place < limit), ext, outside_frame)
        for g in range(groups):
            fr[g] = ext[:, g * GROUP:(g + 1) * GROUP].astype(jnp.float32)

    def local_group(g, carry):
        base = g * GROUP
        key_frame = jnp.broadcast_to(fr[g][0:1, :], (GROUP, GROUP))
        same = (
            lax.broadcasted_iota(jnp.int32, (GROUP, GROUP), 0) // WIN
            == lax.broadcasted_iota(jnp.int32, (GROUP, GROUP), 1) // WIN
        )
        allowed = same & (key_frame <= key_frame.T)
        spans = [slice(i * HD, (i + 1) * HD) for i in range(heads)]
        scores = [
            lax.dot_general(
                q[pl.ds(base, GROUP), span_of], kv[0, pl.ds(base, GROUP), span_of],
                (((1,), (1,)), ((), ())), preferred_element_type=jnp.float32,
            )
            for span_of in spans
        ]
        weights = [jnp.where(allowed, jnp.exp2(score * score_factor), 0.0) for score in scores]
        values = [
            jnp.dot(
                weight.astype(jnp.bfloat16), kv[1, pl.ds(base, GROUP), span_of],
                preferred_element_type=jnp.float32,
            )
            for weight, span_of in zip(weights, spans)
        ]
        for weight, value, span_of in zip(weights, values, spans):
            den[pl.ds(base, GROUP), span_of] = weight
            num[pl.ds(base, GROUP), span_of] = value
        return carry

    def memory_group(g):
        base = g * GROUP
        window = 2 * g
        start = phase * (rows // WIN)
        last = rows // WIN
        first_open = opened[0, start + window]
        second_open = opened[0, start + window + 1] if window + 1 <= last else first_open
        row = lax.broadcasted_iota(jnp.int32, (GROUP, MEM), 0)
        gate = jnp.where(row < WIN, first_open, second_open) == 1
        for i in range(heads):
            span_of = slice(i * HD, (i + 1) * HD)
            score = lax.dot_general(
                q[base:base + GROUP, span_of], mem[0, :, span_of],
                (((1,), (1,)), ((), ())), preferred_element_type=jnp.float32,
            )
            weight = jnp.where(gate, jnp.exp2(score * score_factor), 0.0)
            total = den[base:base + GROUP, span_of]
            for j in range(MEM // HD):
                total = total + weight[:, j * HD:(j + 1) * HD]
            denom = jnp.sum(total, axis=-1, keepdims=True)
            value = num[base:base + GROUP, span_of] + jnp.dot(
                weight.astype(jnp.bfloat16), mem[1, :, span_of],
                preferred_element_type=jnp.float32,
            )
            att[me, base:base + GROUP, span_of] = (value / denom).astype(jnp.bfloat16)

    def work():
        queries()
        frame_rows()
        halo.wait_recv()
        for g in range(groups):
            local_group(g, 0)

    @pl.when(c >= EARLY)
    def _():
        work()

    def relay_rows(first, last):
        for copy, relay in zip(wo_copies[first:last], wo_relays[first:last]):
            copy.wait_recv()
            relay.start()

    early_relays = len(wo_relays) // 2
    relay_rows(0, early_relays)
    for k in range(PIECES):
        chain_piece(k)
    relay_rows(early_relays, len(wo_relays))

    @pl.when(c < EARLY)
    def _():
        work()

    for k in range(PIECES):
        moved[k].wait_recv()

    bounds = [HALF] + [GROUP * g for g in range(1, groups - 1)] + [HALF + rows]
    members = [[g] for g in range(groups - 2)] + [[groups - 2, groups - 1]]
    sides, crosses, relays = [], [], []
    for j, inside in enumerate(members):
        at = pl.ds(bounds[j], bounds[j + 1] - bounds[j])
        for g in inside:
            memory_group(g)
        copy = remote(att.at[me, at], att.at[me, at], a_send.at[j], a_recv.at[j], {"mp": sib})
        copy.start()
        sides.append(copy)
        across, passed = [], []
        for o in range(1, chips):
            to = (me + 2 * o) % n_mp
            source = (me + n_mp - 2 * o) % n_mp
            copy = remote(att.at[me, at], att.at[me, at], c_send.at[j, o - 1], c_recv.at[j, o - 1], {"mp": to})
            copy.start()
            across.append(copy)
            passed.append(remote(
                att.at[source, at], att.at[source, at], r_send.at[j, o - 1], r_recv.at[j, o - 1], {"mp": sib},
            ))
        crosses.append(across)
        relays.append(passed)

    wo_own.wait()
    for copy in wo_relays + wo_middles + [wo_side]:
        copy.wait_recv()

    def finish(j):
        sides[j].wait_recv()
        for copy in relays[j]:
            copy.wait_recv()
        first, count = bounds[j], bounds[j + 1] - bounds[j]
        own = pl.ds(pl.multiple_of(me * share, HD), share)
        total = x[first - HALF:first - HALF + count, own].astype(jnp.float32)
        for m in range(n_mp):
            total = total + jnp.dot(
                att[m, first:first + count, :], wo[m], preferred_element_type=jnp.float32
            )
        out[first - HALF:first - HALF + count, :] = total.astype(jnp.bfloat16)

    for j in range(len(members)):
        for o in range(chips - 1):
            crosses[j][o].wait_recv()
            relays[j][o].start()
        if j > 0:
            finish(j - 1)
    finish(len(members) - 1)

    for copy in wo_copies + wo_middles + wo_relays + tails + moved + sides + [halo, wo_side]:
        copy.wait_send()
    for group in crosses + relays:
        for copy in group:
            copy.wait_send()

    @pl.when(c < n_span - 1)
    def _():
        for copy in chain:
            copy.wait_send()


def local(n_span, n_mp, latents, w_qkv, w_out, decay, frame_ids, memory_mask):
    rows, width = latents.shape
    cols = w_qkv.shape[2]
    share = width // n_mp
    ext = -(-(rows + WIN) // GROUP) * GROUP
    groups = ext // GROUP
    count = groups - 1
    others = max(n_mp // 2 - 1, 1)
    any_spec = pl.BlockSpec(memory_space=pl.ANY)
    vmem_spec = pl.BlockSpec(memory_space=pltpu.VMEM)
    dma = pltpu.SemaphoreType.DMA
    flops = 2 * rows * width * 4 * cols
    return pl.pallas_call(
        functools.partial(body, (n_span, n_mp, rows, width, cols)),
        out_shape=jax.ShapeDtypeStruct((rows, share), jnp.bfloat16),
        in_specs=[any_spec, any_spec, any_spec, vmem_spec, vmem_spec, pl.BlockSpec(memory_space=pltpu.SMEM)],
        out_specs=vmem_spec,
        scratch_shapes=[
            pltpu.VMEM((rows, width), jnp.bfloat16),
            pltpu.VMEM((width, 3 * cols), jnp.bfloat16),
            pltpu.VMEM((n_mp, cols, share), jnp.bfloat16),
            pltpu.VMEM((2, ext, cols), jnp.bfloat16),
            pltpu.VMEM((ext, cols), jnp.bfloat16),
            pltpu.VMEM((ext, cols), jnp.float32),
            pltpu.VMEM((ext, cols), jnp.float32),
            pltpu.VMEM((n_mp, ext, cols), jnp.bfloat16),
            pltpu.VMEM((groups, 8, GROUP), jnp.float32),
            pltpu.VMEM((MEM, cols), jnp.bfloat16),
            pltpu.VMEM((MEM, cols), jnp.bfloat16),
            pltpu.VMEM((MEM, cols), jnp.bfloat16),
            pltpu.VMEM((MEM, cols), jnp.bfloat16),
            pltpu.VMEM((2, MEM, cols), jnp.bfloat16),
            dma((6,)),
            dma, dma,
            dma((2 * others,)), dma((2 * others,)),
            dma((2 * others,)), dma((2 * others,)),
            dma((2 * others,)), dma((2 * others,)),
            dma((PIECES,)), dma((PIECES,)),
            dma((PIECES,)), dma((PIECES,)),
            dma((PIECES,)), dma((PIECES,)),
            dma, dma,
            dma((count,)), dma((count,)),
            dma((count, others)), dma((count, others)),
            dma((count, others)), dma((count, others)),
        ],
        compiler_params=pltpu.CompilerParams(
            collective_id=0, has_side_effects=True, vmem_limit_bytes=60 * 1024 * 1024
        ),
        cost_estimate=pl.CostEstimate(flops=flops, bytes_accessed=12 << 20, transcendentals=1 << 20),
        name="refiner",
    )(
        latents, jnp.transpose(w_qkv, (1, 0, 2)), w_out,
        decay.reshape(decay.shape[1:]), frame_ids, memory_mask,
    )


def solution(mesh):
    return jax.shard_map(
        functools.partial(local, mesh.shape["span"], mesh.shape["mp"]),
        mesh=mesh,
        in_specs=(
            P(("span", "phase"), None),
            P(None, None, "mp"),
            P("mp", None),
            P("span", None, "mp"),
            P("span", None),
            P("span", None),
        ),
        out_specs=P(("span", "phase"), "mp"),
        check_vma=False,
    )
```

profile of v0, /device:TPU:25, one launch (start us, length us, event | category | flops | bytes accessed | tf_op | source)
XLA Modules:
  0.0 36.0 jit_solution(2595701774279924283)
XLA Ops:
  0.0 34.0 %refiner.1 = bf16[512,640]{1,0:T(8,128)(2,1)} custom-call(bf16[512,2560]{1,0:T(8,128)(2,1)} %x_hbm.1, bf16[3,2560,384]{2,1,0:T(8,128)(2,1)} %bitcast.2, bf16[384,2560]{1,0:T(8,128)(2,1)} %wo_hbm.1, f32[2,3]{1,0:T(2,128)} %bitcast.3, s32[1,1024]{1,0:T(1,128)} %frames.1, s32[1,17]{1,0:T(1,128)} %opened.1), custom_call_target="tpu_custom_call" | custom-call | flops 4026531840 | bytes 12582912 | tf_op jit(solution)/shard_map/refiner/pallas_call | solution.py:375
  34.0 2.0 %copy.8 = bf16[512,640]{1,0:T(8,128)(2,1)} copy(bf16[512,640]{1,0:T(8,128)(2,1)} %refiner.1) | data formatting | bytes 1310720
where the time goes:
time: 36.6 us; the launch traced here: 36 us
  Pallas kernels  34 us (93%)
  local copies, waits for them, and re-layouts  1.98 us (5%)
    pallas_call x1, Pallas kernels, local(): pl.pallas_call(functools.partial(body, (n_span, n_mp, rows, width, cols))...  34 us
    unnamed x1, local copies, waits for them, and re-layouts  1.98 us

commit v1 on v0

--- a/solution.py
+++ b/solution.py
@@ -30,8 +30,8 @@
 
 
 def body(
-    sizes, x_hbm, w_hbm, wo_hbm, decay, frames, opened, out,
-    x, w, wo, kv, q, num, den, att, fr, tail_in, s_in, s_out, m_out, mem,
+    sizes, x_hbm, w_hbm, wo_hbm, decay_hbm, frames_hbm, opened_hbm, out,
+    decay, frames, opened, x, w, wo, kv, q, num, den, att, fr, tail_in, s_in, s_out, m_out, mem,
     load_sem, ws_send, ws_recv, wo_send, wo_recv, wm_send, wm_recv, wr_send, wr_recv, y_send, y_recv, z_send, z_recv, m_send, m_recv,
     h_send, h_recv, a_send, a_recv, c_send, c_recv, r_send, r_recv,
 ):
@@ -62,6 +62,8 @@
     x_head = load(3, x_hbm.at[pl.ds(0, top)], x.at[pl.ds(0, top)])
     w_query = load(4, w_hbm.at[0], w.at[:, pl.ds(2 * cols, cols)])
     wo_own = load(5, wo_hbm.at[:, pl.ds(pl.multiple_of(me * share, HD), share)], wo.at[me])
+
+    small = [load(6, decay_hbm, decay), load(7, frames_hbm, frames), load(8, opened_hbm, opened)]
 
     barrier = pltpu.get_barrier_semaphore()
     for o in range(1, n_mp):
@@ -137,6 +139,8 @@
 
     x_tail.wait()
     w_sent.wait()
+    for copy in small:
+        copy.wait()
     kv[sent, tail0:tail0 + MEM, :] = unit(project(top, MEM, 0), sent == 0)
     tails, chain, moved = [], [], []
     for k in range(PIECES):
@@ -368,16 +372,19 @@
     groups = ext // GROUP
     count = groups - 1
     others = max(n_mp // 2 - 1, 1)
-    any_spec = pl.BlockSpec(memory_space=pl.ANY)
+    any_spec = pl.BlockSpec(memory_space=pltpu.HBM)
     vmem_spec = pl.BlockSpec(memory_space=pltpu.VMEM)
     dma = pltpu.SemaphoreType.DMA
     flops = 2 * rows * width * 4 * cols
     return pl.pallas_call(
         functools.partial(body, (n_span, n_mp, rows, width, cols)),
         out_shape=jax.ShapeDtypeStruct((rows, share), jnp.bfloat16),
-        in_specs=[any_spec, any_spec, any_spec, vmem_spec, vmem_spec, pl.BlockSpec(memory_space=pltpu.SMEM)],
+        in_specs=[any_spec] * 6,
         out_specs=vmem_spec,
         scratch_shapes=[
+            pltpu.VMEM(decay.shape[1:], jnp.float32),
+            pltpu.VMEM(frame_ids.shape, jnp.int32),
+            pltpu.SMEM(memory_mask.shape, jnp.int32),
             pltpu.VMEM((rows, width), jnp.bfloat16),
             pltpu.VMEM((width, 3 * cols), jnp.bfloat16),
             pltpu.VMEM((n_mp, cols, share), jnp.bfloat16),
@@ -392,7 +399,7 @@
             pltpu.VMEM((MEM, cols), jnp.bfloat16),
             pltpu.VMEM((MEM, cols), jnp.bfloat16),
             pltpu.VMEM((2, MEM, cols), jnp.bfloat16),
-            dma((6,)),
+            dma((9,)),
             dma, dma,
             dma((2 * others,)), dma((2 * others,)),
             dma((2 * others,)), dma((2 * others,)),
@@ -406,13 +413,13 @@
             dma((count, others)), dma((count, others)),
         ],
         compiler_params=pltpu.CompilerParams(
-            collective_id=0, has_side_effects=True, vmem_limit_bytes=60 * 1024 * 1024
+            collective_id=0, has_side_effects=True, vmem_limit_bytes=40 * 1024 * 1024
         ),
         cost_estimate=pl.CostEstimate(flops=flops, bytes_accessed=12 << 20, transcendentals=1 << 20),
         name="refiner",
     )(
-        latents, jnp.transpose(w_qkv, (1, 0, 2)), w_out,
-        decay.reshape(decay.shape[1:]), frame_ids, memory_mask,
+        *[pltpu.with_memory_space_constraint(a, pltpu.HBM) for a in (latents, jnp.transpose(w_qkv, (1, 0, 2)), w_out,
+        decay.reshape(decay.shape[1:]), frame_ids, memory_mask)]
     )
 
 

time: 36.6 us -> 35.1 us (0.959); the launches traced: 36 us -> 35 us
  local copies, waits for them, and re-layouts: 1.98 us -> 0.84 us
    unnamed x1, local copies, waits for them, and re-layouts: 1.98 us -> 0.84 us
where the time goes in v1:
time: 35.1 us; the launch traced here: 35 us
  Pallas kernels  34.1 us (97%)
  local copies, waits for them, and re-layouts  0.84 us (2%)
    pallas_call x1, Pallas kernels, local(): pl.pallas_call(functools.partial(body, (n_span, n_mp, rows, width, cols))...  34.1 us
    unnamed x1, local copies, waits for them, and re-layouts  0.84 us

profile of v1, /device:TPU:25, one launch (start us, length us, event | category | flops | bytes accessed | tf_op | source)
XLA Modules:
  0.0 35.0 jit_solution(6473807294755016847)
XLA Ops:
  0.0 34.1 %refiner.1 = bf16[512,640]{1,0:T(8,128)(2,1)S(1)} custom-call(bf16[512,2560]{1,0:T(8,128)(2,1)} %x_hbm.1, bf16[3,2560,384]{2,1,0:T(8,128)(2,1)} %bitcast.2, bf16[384,2560]{1,0:T(8,128)(2,1)} %wo_hbm.1, f32[2,3]{1,0:T(2,128)} %bitcast.3, s32[1,1024]{1,0:T(1,128)} %frames_hbm.1, s32[1,17]{1,0:T(1,128)} %opened_hbm.1), custom_call_target="tpu_custom_call" | custom-call | flops 4026531840 | bytes 12582912 | tf_op jit(solution)/shard_map/refiner/pallas_call | solution.py:379
  34.1 0.8 %copy.8 = bf16[512,640]{1,0:T(8,128)(2,1)} copy(bf16[512,640]{1,0:T(8,128)(2,1)S(1)} %refiner.1) | data formatting | bytes 1310720

commit v2 on v1

v2 whole, which is shorter than its diff:
```python
import contextlib
import functools
import math

import jax
import jax.numpy as jnp
from jax import lax
from jax.experimental import pallas as pl
from jax.experimental.pallas import tpu as pltpu
from jax.sharding import PartitionSpec as P

HD = 128
WIN = 64
MEM = 256
HALF = WIN // 2
GROUP = 128
CUTS = 4
KPARTS = 4
PLAN = ((0, 1, 2), (1, 2, 3), (2, 3, 5), (3, 4, 6))
MESH = pl.DeviceIdType.MESH

outside_frame = 1048576
epsilon = 1e-06
score_factor = HD ** (-0.5) * math.log2(math.e)


@contextlib.contextmanager
def scope(name):
    yield


def remote(src, dst, send, recv, where):
    return pltpu.make_async_remote_copy(
        src_ref=src, dst_ref=dst, send_sem=send, recv_sem=recv,
        device_id=where, device_id_type=MESH,
    )


def body(
    sizes, x_hbm, w_hbm, wo_hbm, decay_hbm, frames_hbm, opened_hbm, out,
    decay, frames, opened, x, w, wo, kv, q, num, den, att, acc, fr, tail_in, s_in, s_out, m_out, mem,
    load_sem, ws_send, ws_recv, wo_send, wo_recv, wd_send, wu_send, wr_recv, y_send, y_recv, z_send, z_recv, m_send, m_recv,
    h_send, h_recv, a_send, a_recv, c_send, c_recv, r_send, r_recv,
):
    n_span, n_mp, rows, width, cols = sizes
    heads = cols // HD
    share = width // n_mp
    groups = kv.shape[2] // GROUP
    c = lax.axis_index("span")
    me = lax.axis_index("mp")
    phase = lax.axis_index("phase")
    is0 = phase == 0
    other = 1 - phase
    kept, sent = phase, 1 - phase
    sib = me + 1 - 2 * (me % 2)
    chips = n_mp // 2
    top = rows - MEM
    tail0 = HALF + top
    piece = MEM // CUTS
    last = n_span - 1

    barrier = pltpu.get_barrier_semaphore()
    for o in range(1, n_mp):
        pl.semaphore_signal(barrier, inc=1, device_id={"mp": (me + o) % n_mp}, device_id_type=MESH)
    pl.semaphore_signal(barrier, inc=1, device_id={"phase": other}, device_id_type=MESH)

    @pl.when(c > 0)
    def _():
        pl.semaphore_signal(barrier, inc=1, device_id={"span": c - 1}, device_id_type=MESH)

    @pl.when(c < last)
    def _():
        pl.semaphore_signal(barrier, inc=1, device_id={"span": c + 1}, device_id_type=MESH)

    def load(i, src, dst):
        copy = pltpu.make_async_copy(src, dst, load_sem.at[i])
        copy.start()
        return copy

    deep = width // KPARTS
    for n in range(KPARTS):
        at = pl.ds(n * deep, deep)
        load(n, x_hbm.at[pl.ds(top, MEM), at], x.at[pl.ds(top, MEM), at])
        load(n, w_hbm.at[1 + sent, at], w.at[at, pl.ds(0, cols)])
    late = KPARTS
    both_parts = w.at[pl.ds(0, deep), pl.ds(0, MEM + cols)]

    zero_rows = kv.shape[2] - (HALF + rows + HALF)
    kv[:, :, HALF + rows + HALF:, :] = jnp.zeros((2, heads, zero_rows, HD), jnp.bfloat16)
    q[:, HALF + rows:, :] = jnp.zeros((heads, q.shape[1] - HALF - rows, HD), jnp.bfloat16)
    q[:, :HALF, :] = jnp.zeros((heads, HALF, HD), jnp.bfloat16)
    blank = pl.multiple_of(phase * (HALF + rows), HALF)
    kv[:, :, pl.ds(blank, HALF), :] = jnp.zeros((2, heads, HALF, HD), jnp.bfloat16)

    @pl.when(c == 0)
    def _():
        s_in[...] = jnp.zeros(s_in.shape, s_in.dtype)

    block = HD // 2
    parity = (c + phase) % 2

    def columns_of(m):
        return pl.ds(pl.multiple_of(m * share, HD), share)

    wo_copies, wo_downs, wo_ups, wo_acrosses, far = [], [], [], [], []
    for o in range(1, chips):
        for near in (me, sib):
            far.append((near + n_mp - 2 * o) % n_mp)
    for i in range(heads):
        part = pl.ds(pl.multiple_of(i * HD + parity * block, block), block)
        for o in range(1, chips):
            for near in (me, sib):
                to, source = (near + 2 * o) % n_mp, (near + n_mp - 2 * o) % n_mp
                at = len(wo_copies)
                wo_copies.append(remote(
                    wo_hbm.at[part, columns_of(to)], wo.at[me, part],
                    wo_send, wo_recv.at[at], {"mp": to},
                ))
                held = wo.at[source, part]
                wo_downs.append(remote(held, held, wd_send, wr_recv.at[i], {"span": (c + last) % n_span}))
                if i == 0:
                    wo_acrosses.append(remote(held, held, wu_send, wr_recv.at[i], {"phase": other}))
                else:
                    wo_ups.append(remote(held, held, wu_send, wr_recv.at[i], {"span": (c + 1) % n_span}))
    wo_side = remote(wo_hbm.at[:, columns_of(sib)], wo.at[me], ws_send, ws_recv, {"mp": sib})
    per_head = len(far)

    def relay(at):
        with scope("relay"):
            wo_copies[at].wait_recv()

        @pl.when(c > 0)
        def _():
            wo_downs[at].start()

        if at < per_head:
            @pl.when(c == last)
            def _():
                wo_acrosses[at].start()

    def relay_up(first, end):
        @pl.when(c == last - 1)
        def _():
            for at in range(first, end):
                wo_ups[at - per_head].start()

    def unit(part, flag):
        scale = lax.rsqrt(jnp.mean(part * part, axis=-1, keepdims=True) + epsilon)
        if flag is not None:
            scale = jnp.where(flag, scale, 1.0)
        return (part * scale).astype(jnp.bfloat16)

    def project(first, count, column, size):
        return jnp.dot(
            x[first:first + count, :], w[:, column:column + size],
            preferred_element_type=jnp.float32,
        )

    def tail_copy(k, i, r):
        return remote(
            kv.at[sent, i, pl.ds(tail0 + r * piece, piece)], tail_in.at[i, pl.ds(r * piece, piece)],
            y_send, y_recv.at[k], {"phase": other},
        )

    def chain_copy(k, i, r):
        at = pl.ds(r * piece, piece)
        return remote(s_out.at[i, at], s_in.at[i, at], z_send, z_recv.at[k], {"span": (c + 1) % n_span})

    def moved_copy(k, i, r):
        at = pl.ds(r * piece, piece)
        return remote(m_out.at[i, at], mem.at[kept, i, at], m_send, m_recv.at[i], {"phase": other})

    def each(make):
        return [make(i * CUTS + r, i, r) for i in range(heads) for r in range(CUTS)]

    tails = each(tail_copy)

    def keep(raw, first, count, n, at):
        which = sent if n < heads else kept
        part = raw[:, at * HD:(at + 1) * HD]
        kv[which, n % heads, HALF + first:HALF + first + count, :] = unit(part, which == 0)

    def send_tail(i):
        for r in range(CUTS):
            tails[i * CUTS + r].start()

    raw = None
    for n in range(KPARTS):
        with scope("load%d" % n):
            pltpu.make_async_copy(both_parts, both_parts, load_sem.at[n]).wait()
        if n == 0:
            w_kept = load(late, w_hbm.at[1 + kept], w.at[:, pl.ds(cols, cols)])
        if n == 1:
            small = [
                load(late + 1, decay_hbm, decay), load(late + 2, frames_hbm, frames),
                load(late + 3, opened_hbm, opened),
            ]
            x_head = load(late + 4, x_hbm.at[pl.ds(0, top)], x.at[pl.ds(0, top)])
        if n == KPARTS - 1:
            with scope("bar"):
                pl.semaphore_wait(barrier, n_mp + 1 + (c + n_span - 1) // n_span - (c + 1) // n_span)
            for copy in wo_copies:
                copy.start()
        at = slice(n * deep, (n + 1) * deep)
        with scope("sent%d" % n):
            step = jnp.dot(x[top:, at], w[at, :HD], preferred_element_type=jnp.float32)
            raw = step if raw is None else raw + step
    with scope("unit"):
        keep(raw, top, MEM, 0, 0)
    send_tail(0)
    wo_side.start()
    w_query = load(late + 5, w_hbm.at[0], w.at[:, pl.ds(2 * cols, cols)])
    wo_own = load(late + 6, wo_hbm.at[:, columns_of(me)], wo.at[me])
    with scope("sentrest"):
        raw = project(top, MEM, HD, cols - HD)
        for i in range(1, heads):
            keep(raw, top, MEM, i, i - 1)
    with scope("loadk"):
        w_kept.wait()
    with scope("kept"):
        raw = project(top, MEM, cols, cols)
        for i in range(heads):
            keep(raw, top, MEM, heads + i, i)
    with scope("loadh"):
        x_head.wait()

    def head_rows(pair):
        with scope("headkv"):
            raw = project(0, top, pair * HD, 2 * HD)
            for at in range(2):
                keep(raw, 0, top, pair + at, at)

    for copy in small:
        copy.wait()
    halo_from = pl.multiple_of(HALF + other * (rows - HALF), HALF)
    halo = remote(
        kv.at[:, :, pl.ds(halo_from, HALF)], kv.at[:, :, pl.ds(blank, HALF)],
        h_send, h_recv, {"phase": other},
    )

    def rate_of(half, i):
        rate = decay[half:half + 1, 0:1]
        for n in range(1, heads):
            rate = jnp.where(i == n, decay[half:half + 1, n:n + 1], rate)
        return jnp.broadcast_to(rate, (1, HD))

    def mix(rate):
        return jnp.where(is0, 1.0 - rate, jnp.sqrt(1.0 - rate * rate))

    def chain_head(i):
        r0, r1 = rate_of(0, i), rate_of(1, i)
        f0, f1, both = mix(r0), mix(r1), r0 * r1
        for r in range(CUTS):
            k = i * CUTS + r
            rows_at = pl.ds(r * piece, piece)
            own = kv[kept, i, tail0 + r * piece:tail0 + (r + 1) * piece, :].astype(jnp.float32)
            with scope("waittail"):
                tail_copy(k, i, r).wait_recv()
            theirs = tail_in[i, rows_at, :].astype(jnp.float32)
            low = f0 * jnp.where(is0, own, theirs)
            high = r1 * low + f1 * jnp.where(is0, theirs, own)

            @pl.when(c > 0)
            def _():
                with scope("waitchain"):
                    chain_copy(k, i, r).wait_recv()

            state = s_in[i, rows_at, :].astype(jnp.float32)
            s_out[i, rows_at, :] = (both * state + high).astype(jnp.bfloat16)

            @pl.when(c < last)
            def _():
                chain_copy(k, i, r).start()

            later = r0 * state + low
            m_out[i, rows_at, :] = jnp.where(is0, later, state).astype(jnp.bfloat16)
            moved_copy(k, i, r).start()
            mem[kept, i, rows_at, :] = jnp.where(is0, state, later).astype(jnp.bfloat16)

    def queries(first, count):
        with scope("queries"):
            raw = project(first, count, 2 * cols, cols)
            for i in range(heads):
                q[i, HALF + first:HALF + first + count, :] = unit(raw[:, i * HD:(i + 1) * HD], None)

    def frame_rows():
        total = frames.shape[1]
        wide = jnp.broadcast_to(frames[...], (8, total))
        ahead = pltpu.roll(wide, HALF, 1)
        behind = pltpu.roll(wide, total - (rows - HALF), 1)
        place = lax.broadcasted_iota(jnp.int32, wide.shape, 1)
        ext = jnp.where(is0, ahead, behind)
        least = jnp.where(is0, HALF, 0)
        limit = jnp.where(is0, total + HALF, rows + HALF)
        ext = jnp.where((place >= least) & (place < limit), ext, outside_frame)
        for g in range(groups):
            fr[g] = ext[:, g * GROUP:(g + 1) * GROUP].astype(jnp.float32)

    def local_group(g):
        at = pl.ds(g * GROUP, GROUP)
        key_frame = jnp.broadcast_to(fr[g][0:1, :], (GROUP, GROUP))
        same = (
            lax.broadcasted_iota(jnp.int32, (GROUP, GROUP), 0) // WIN
            == lax.broadcasted_iota(jnp.int32, (GROUP, GROUP), 1) // WIN
        )
        allowed = same & (key_frame <= key_frame.T)
        scores = [
            lax.dot_general(
                q[i, at, :], kv[0, i, at, :],
                (((1,), (1,)), ((), ())), preferred_element_type=jnp.float32,
            )
            for i in range(heads)
        ]
        weights = [jnp.where(allowed, jnp.exp2(score * score_factor), 0.0) for score in scores]
        values = [
            jnp.dot(weights[i].astype(jnp.bfloat16), kv[1, i, at, :], preferred_element_type=jnp.float32)
            for i in range(heads)
        ]
        for i in range(heads):
            den[i, at, :] = weights[i]
            num[i, at, :] = values[i]

    spots = [(i, n * 2 * GROUP, 2 * GROUP) for i in range(heads - 1) for n in range(rows // (2 * GROUP))]
    spots += [(heads - 1, n * GROUP, GROUP) for n in range(rows // GROUP)]
    sides, crosses, relays = [], [], []
    for j, (i, first, count) in enumerate(spots):
        at = pl.ds(first, count)
        mine = att.at[me, i, at]
        sides.append(remote(mine, mine, a_send, a_recv, {"mp": sib}))
        across, passed = [], []
        for o in range(1, chips):
            to = (me + 2 * o) % n_mp
            theirs = att.at[(me + n_mp - 2 * o) % n_mp, i, at]
            across.append(remote(mine, mine, c_send, c_recv.at[j, o - 1], {"mp": to}))
            passed.append(remote(theirs, theirs, r_send, r_recv.at[max(j - len(spots) + rows // GROUP + 1, 0)], {"mp": sib}))
        crosses.append(across)
        relays.append(passed)

    start = phase * (rows // WIN)

    def memory_groups(i, members):
        scores, flagged = [], []
        for g in members:
            window = start + g * (GROUP // WIN)
            row = lax.broadcasted_iota(jnp.int32, (GROUP, MEM), 0)
            flags = opened[0, window + GROUP // WIN]
            for n in range(GROUP // WIN - 1, -1, -1):
                flags = jnp.where(row < HALF + n * WIN, opened[0, window + n], flags)
            flagged.append(flags == 1)
            scores.append(lax.dot_general(
                q[i, HALF + g * GROUP:HALF + (g + 1) * GROUP, :], mem[0, i],
                (((1,), (1,)), ((), ())), preferred_element_type=jnp.float32,
            ))
        weights = [
            jnp.where(flags, jnp.exp2(score * score_factor), 0.0) for score, flags in zip(scores, flagged)
        ]
        values = [
            jnp.dot(weight.astype(jnp.bfloat16), mem[1, i], preferred_element_type=jnp.float32)
            for weight in weights
        ]
        for g, weight, value in zip(members, weights, values):
            at = slice(HALF + g * GROUP, HALF + (g + 1) * GROUP)
            total = den[i, at, :]
            for j in range(MEM // HD):
                total = total + weight[:, j * HD:(j + 1) * HD]
            denom = jnp.sum(total, axis=-1, keepdims=True)
            att[me, i, g * GROUP:(g + 1) * GROUP, :] = ((num[i, at, :] + value) / denom).astype(jnp.bfloat16)

    def memory_head(i):
        with scope("waitmem"):
            remote(m_out.at[i], mem.at[kept, i], m_send, m_recv.at[i], {"phase": other}).wait_recv()
        with scope("mem"):
            for base in range(0, rows, 2 * GROUP):
                memory_groups(i, [base // GROUP, base // GROUP + 1])
                for j, (which, first, count) in enumerate(spots):
                    if which == i and base <= first < base + 2 * GROUP:
                        for copy in crosses[j]:
                            copy.start()
                        sides[j].start()

    def relay_head(i, n):
        for at in range(i * per_head + n * per_head // 2, i * per_head + (n + 1) * per_head // 2):
            relay(at)

    end = heads * per_head
    plan = {}
    for kind, spots_of in enumerate(PLAN):
        for i, place in enumerate(spots_of):
            plan.setdefault(place, []).append((kind, i))

    def chain_at(place):
        kind, i = jnp.minimum(c, len(PLAN) - 1), jnp.int32(heads)
        for which, head in plan[place]:
            if head < heads:
                i = jnp.where(kind == which, head, i)

        @pl.when(i < heads)
        def _():
            with scope("chain%d" % place):
                chain_head(i)

    for pair in range(0, 2 * heads, 2):
        head_rows(pair)
        if pair == 0:
            send_tail(1)
    halo.start()
    chain_at(0)
    with scope("loadq"):
        w_query.wait()
    queries(0, top)
    for i in range(2, heads):
        send_tail(i)
    relay_head(0, 0)
    queries(top, rows - top)
    chain_at(1)
    relay_head(0, 1)
    with scope("local"):
        frame_rows()
        for g in range(1, groups - 1):
            local_group(g)
        with scope("halo"):
            halo.wait_recv()
        local_group(0)
        local_group(groups - 1)
    chain_at(2)
    relay_head(1, 0)
    chain_at(3)
    relay_head(1, 1)
    chain_at(4)
    relay_head(2, 0)
    memory_head(0)
    chain_at(5)
    relay_up(per_head, 2 * per_head + per_head // 2)
    chain_at(6)
    relay_head(2, 1)
    memory_head(1)
    relay_up(2 * per_head + per_head // 2, heads * per_head)
    memory_head(2)

    own = pl.ds(pl.multiple_of(me * share, HD), share)

    def product(sources, which, first, count):
        left = jnp.concatenate([att[m, i, first:first + count, :] for m in sources for i in which], axis=1)
        right = jnp.concatenate([wo[m, i * HD:(i + 1) * HD, :] for m in sources for i in which], axis=0)
        return jnp.dot(left, right, preferred_element_type=jnp.float32)

    def add(sources, which, scope_name):
        with scope(scope_name):
            for first in range(0, rows, 2 * GROUP):
                at = slice(first, first + 2 * GROUP)
                acc[at, :] = acc[at, :] + product(sources, which, first, 2 * GROUP)

    def cross(j):
        for o in range(chips - 1):
            with scope("waitcross"):
                crosses[j][o].wait_recv()
            relays[j][o].start()

    def arrived(lot, which):
        with scope("waitrelay"):
            remote(lot, lot, r_send, r_recv.at[which], {"mp": sib}).wait_recv()

    def far_weights(i):
        with scope("waitwo"):
            lot = wo.at[pl.ds(0, chips - 1), pl.ds(0, HD)]
            remote(lot, lot, wd_send, wr_recv.at[i], {"phase": other}).wait_recv()

    order = [[j for j, spot in enumerate(spots) if spot[0] == i] for i in range(heads)]
    wo_own.wait()
    with scope("own"):
        for first in range(0, rows, 2 * GROUP):
            at = slice(first, first + 2 * GROUP)
            acc[at, :] = x[at, own].astype(jnp.float32) + product([me], range(heads), first, 2 * GROUP)
    early = range(heads - 1)
    for i in early:
        for j in order[i]:
            cross(j)
    with scope("waitside"):
        wo_side.wait_recv()
        remote(att.at[me], att.at[me], a_send, a_recv, {"mp": sib}).wait_recv()
    add([sib], range(heads), "near")
    for i in early:
        far_weights(i)
    add(far[0::2], early, "direct")
    final = order[heads - 1]
    for j in final[:2]:
        cross(j)
    arrived(att.at[pl.ds(0, chips - 1), pl.ds(0, heads - 1)], 0)
    add(far[1::2], early, "passed")
    far_weights(heads - 1)
    for n, j in enumerate(final):
        if n + 2 < len(final):
            cross(final[n + 2])
        first, count = spots[j][1], spots[j][2]
        arrived(att.at[pl.ds(0, chips - 1), heads - 1, pl.ds(first, count)], 1 + n)
        with scope("fin"):
            at = slice(first, first + count)
            out[at, :] = (acc[at, :] + product(far, [heads - 1], first, count)).astype(jnp.bfloat16)

    with scope("sends"):
        tail_all = kv.at[sent, :, pl.ds(tail0, MEM)]
        wo_all = wo.at[pl.ds(0, chips - 1)]
        att_all = att.at[pl.ds(0, chips - 1)]
        for src, send, recv, where in (
            (tail_all, y_send, y_recv.at[0], {"phase": other}),
            (m_out, m_send, m_recv.at[0], {"phase": other}),
            (wo_all, wo_send, wo_recv.at[0], {"mp": sib}),
            (att.at[me], a_send, a_recv, {"mp": sib}),
            (att_all, c_send, c_recv.at[0, 0], {"mp": sib}),
            (att_all, r_send, r_recv.at[0], {"mp": sib}),
        ):
            remote(src, src, send, recv, where).wait_send()
        halo.wait_send()
        wo_side.wait_send()

        @pl.when(c < last)
        def _():
            remote(s_out, s_in, z_send, z_recv.at[0], {"phase": other}).wait_send()

        @pl.when(c > 0)
        def _():
            remote(wo_all, wo_all, wd_send, wr_recv.at[0], {"phase": other}).wait_send()

        @pl.when(c == last - 1)
        def _():
            lot = wo.at[pl.ds(0, chips - 1), pl.ds(0, (heads - 1) * HD)]
            remote(lot, lot, wu_send, wr_recv.at[0], {"phase": other}).wait_send()

        @pl.when(c == last)
        def _():
            lot = wo.at[pl.ds(0, chips - 1), pl.ds(0, HD)]
            remote(lot, lot, wu_send, wr_recv.at[0], {"phase": other}).wait_send()


def local(n_span, n_mp, latents, w_qkv, w_out, decay, frame_ids, memory_mask):
    rows, width = latents.shape
    cols = w_qkv.shape[2]
    heads = cols // HD
    share = width // n_mp
    ext = -(-(rows + WIN) // GROUP) * GROUP
    groups = ext // GROUP
    others = max(n_mp // 2 - 1, 1)
    chunks = 2 * others * heads
    pieces = heads * CUTS
    spots = (heads - 1) * (rows // (2 * GROUP)) + rows // GROUP
    hbm_spec = pl.BlockSpec(memory_space=pltpu.HBM)
    dma = pltpu.SemaphoreType.DMA
    bf16, f32 = jnp.bfloat16, jnp.float32
    flops = 2 * rows * width * 4 * cols
    inputs = (
        latents, jnp.transpose(w_qkv, (1, 0, 2)), w_out,
        decay.reshape(decay.shape[1:]), frame_ids, memory_mask,
    )
    return pl.pallas_call(
        functools.partial(body, (n_span, n_mp, rows, width, cols)),
        out_shape=jax.ShapeDtypeStruct((rows, share), bf16),
        in_specs=[hbm_spec] * 6,
        out_specs=pl.BlockSpec(memory_space=pltpu.VMEM),
        scratch_shapes=[
            pltpu.VMEM(decay.shape[1:], f32),
            pltpu.VMEM(frame_ids.shape, jnp.int32),
            pltpu.SMEM(memory_mask.shape, jnp.int32),
            pltpu.VMEM((rows, width), bf16),
            pltpu.VMEM((width, 3 * cols), bf16),
            pltpu.VMEM((n_mp, cols, share), bf16),
            pltpu.VMEM((2, heads, ext, HD), bf16),
            pltpu.VMEM((heads, ext, HD), bf16),
            pltpu.VMEM((heads, ext, HD), f32),
            pltpu.VMEM((heads, ext, HD), f32),
            pltpu.VMEM((n_mp, heads, rows, HD), bf16),
            pltpu.VMEM((rows, share), f32),
            pltpu.VMEM((groups, 8, GROUP), f32),
            pltpu.VMEM((heads, MEM, HD), bf16),
            pltpu.VMEM((heads, MEM, HD), bf16),
            pltpu.VMEM((heads, MEM, HD), bf16),
            pltpu.VMEM((heads, MEM, HD), bf16),
            pltpu.VMEM((2, heads, MEM, HD), bf16),
            dma((KPARTS + 7,)),
            dma, dma,
            dma, dma((chunks,)), dma, dma, dma((heads,)),
            dma, dma((pieces,)),
            dma, dma((pieces,)),
            dma, dma((heads,)),
            dma, dma,
            dma, dma,
            dma, dma((spots, others)),
            dma, dma((1 + rows // GROUP,)),
        ],
        compiler_params=pltpu.CompilerParams(
            collective_id=0, has_side_effects=True, vmem_limit_bytes=40 * 1024 * 1024
        ),
        cost_estimate=pl.CostEstimate(flops=flops, bytes_accessed=12 << 20, transcendentals=1 << 20),
        name="refiner",
    )(*[pltpu.with_memory_space_constraint(a, pltpu.HBM) for a in inputs])


def solution(mesh):
    return jax.shard_map(
        functools.partial(local, mesh.shape["span"], mesh.shape["mp"]),
        mesh=mesh,
        in_specs=(
            P(("span", "phase"), None),
            P(None, None, "mp"),
            P("mp", None),
            P("span", None, "mp"),
            P("span", None),
            P("span", None),
        ),
        out_specs=P(("span", "phase"), "mp"),
        check_vma=False,
    )
```

time: 35.1 us -> 31.2 us (0.89)
  Pallas kernels: 34.1 us -> 30.2 us
    pallas_call x1, Pallas kernels: 34.1 us -> 30.2 us  [local(): pl.pallas_call(functools.partial(body, (n_span, n_mp, rows, width, cols))...]
where the time goes in v2:
time: 31.2 us; the launch traced here: 31 us
  Pallas kernels  30.2 us (97%)
  local copies, waits for them, and re-layouts  0.84 us (3%)
    pallas_call x1, Pallas kernels, local(): pl.pallas_call(functools.partial(body, (n_span, n_mp, rows, width, cols))...  30.2 us
    unnamed x1, local copies, waits for them, and re-layouts  0.84 us

profile of v2, /device:TPU:25, one launch (start us, length us, event | category | flops | bytes accessed | tf_op | source)
XLA Modules:
  0.0 31.0 jit_solution(14070708673267105496)
XLA Ops:
  0.0 30.2 %refiner.1 = bf16[512,640]{1,0:T(8,128)(2,1)S(1)} custom-call(bf16[512,2560]{1,0:T(8,128)(2,1)} %x_hbm.1, bf16[3,2560,384]{2,1,0:T(8,128)(2,1)} %bitcast.2, bf16[384,2560]{1,0:T(8,128)(2,1)} %wo_hbm.1, f32[2,3]{1,0:T(2,128)} %bitcast.3, s32[1,1024]{1,0:T(1,128)} %frames_hbm.1, s32[1,17]{1,0:T(1,128)} %opened_hbm.1), custom_call_target="tpu_custom_call" | custom-call | flops 4026531840 | bytes 12582912 | tf_op jit(solution)/shard_map/refiner/pallas_call | solution.py:554
  30.2 0.8 %copy.8 = bf16[512,640]{1,0:T(8,128)(2,1)} copy(bf16[512,640]{1,0:T(8,128)(2,1)S(1)} %refiner.1) | data formatting | bytes 1310720

commit v3 on v2

--- a/solution.py
+++ b/solution.py
@@ -15,8 +15,8 @@
 HALF = WIN // 2
 GROUP = 128
 CUTS = 4
-KPARTS = 4
-PLAN = ((0, 1, 2), (1, 2, 3), (2, 3, 5), (3, 4, 6))
+KPARTS = 2
+PLAN = ((0, 1, 3), (2, 4, 5), (4, 5, 6), (5, 6, 7))
 MESH = pl.DeviceIdType.MESH
 
 outside_frame = 1048576
@@ -81,9 +81,16 @@
     for n in range(KPARTS):
         at = pl.ds(n * deep, deep)
         load(n, x_hbm.at[pl.ds(top, MEM), at], x.at[pl.ds(top, MEM), at])
-        load(n, w_hbm.at[1 + sent, at], w.at[at, pl.ds(0, cols)])
-    late = KPARTS
-    both_parts = w.at[pl.ds(0, deep), pl.ds(0, MEM + cols)]
+        load(n, w_hbm.at[1 + sent, at, pl.ds(0, HD)], w.at[at, pl.ds(0, HD)])
+    both_parts = w.at[pl.ds(0, deep), pl.ds(0, MEM + HD)]
+    w_sent = load(KPARTS, w_hbm.at[1 + sent, :, pl.ds(HD, cols - HD)], w.at[:, pl.ds(HD, cols - HD)])
+    w_kept = load(KPARTS + 1, w_hbm.at[1 + kept], w.at[:, pl.ds(cols, cols)])
+    w_query = load(KPARTS + 2, w_hbm.at[0], w.at[:, pl.ds(2 * cols, cols)])
+    small = [
+        load(KPARTS + 3, decay_hbm, decay), load(KPARTS + 4, frames_hbm, frames), load(KPARTS + 5, opened_hbm, opened),
+    ]
+    x_head = load(KPARTS + 6, x_hbm.at[pl.ds(0, top)], x.at[pl.ds(0, top)])
+    wo_own = load(KPARTS + 7, wo_hbm.at[:, pl.ds(pl.multiple_of(me * share, HD), share)], wo.at[me])
 
     zero_rows = kv.shape[2] - (HALF + rows + HALF)
     kv[:, :, HALF + rows + HALF:, :] = jnp.zeros((2, heads, zero_rows, HD), jnp.bfloat16)
@@ -102,7 +109,8 @@
     def columns_of(m):
         return pl.ds(pl.multiple_of(m * share, HD), share)
 
-    wo_copies, wo_downs, wo_ups, wo_acrosses, far = [], [], [], [], []
+    wo_copies, wo_downs, wo_ups, wo_acrosses, far = [], [], {}, [], []
+    acrosses = range(chips - 1, 2 * (chips - 1))
     for o in range(1, chips):
         for near in (me, sib):
             far.append((near + n_mp - 2 * o) % n_mp)
@@ -118,10 +126,10 @@
                 ))
                 held = wo.at[source, part]
                 wo_downs.append(remote(held, held, wd_send, wr_recv.at[i], {"span": (c + last) % n_span}))
-                if i == 0:
+                if at in acrosses:
                     wo_acrosses.append(remote(held, held, wu_send, wr_recv.at[i], {"phase": other}))
                 else:
-                    wo_ups.append(remote(held, held, wu_send, wr_recv.at[i], {"span": (c + 1) % n_span}))
+                    wo_ups[at] = remote(held, held, wu_send, wr_recv.at[i], {"span": (c + 1) % n_span})
     wo_side = remote(wo_hbm.at[:, columns_of(sib)], wo.at[me], ws_send, ws_recv, {"mp": sib})
     per_head = len(far)
 
@@ -133,16 +141,16 @@
         def _():
             wo_downs[at].start()
 
-        if at < per_head:
+        if at in acrosses:
             @pl.when(c == last)
             def _():
-                wo_acrosses[at].start()
+                wo_acrosses[at - acrosses[0]].start()
 
     def relay_up(first, end):
         @pl.when(c == last - 1)
         def _():
             for at in range(first, end):
-                wo_ups[at - per_head].start()
+                wo_ups[at].start()
 
     def unit(part, flag):
         scale = lax.rsqrt(jnp.mean(part * part, axis=-1, keepdims=True) + epsilon)
@@ -176,62 +184,66 @@
     tails = each(tail_copy)
 
     def keep(raw, first, count, n, at):
-        which = sent if n < heads else kept
         part = raw[:, at * HD:(at + 1) * HD]
-        kv[which, n % heads, HALF + first:HALF + first + count, :] = unit(part, which == 0)
+        rows_at = slice(HALF + first, HALF + first + count)
+        if n >= 2 * heads:
+            q[n - 2 * heads, rows_at, :] = unit(part, None)
+        else:
+            which = sent if n < heads else kept
+            kv[which, n % heads, rows_at, :] = unit(part, which == 0)
+
+    def columns(first, count, n, end):
+        raw = project(first, count, n * HD, (end - n) * HD)
+        for at in range(end - n):
+            keep(raw, first, count, n + at, at)
 
     def send_tail(i):
         for r in range(CUTS):
             tails[i * CUTS + r].start()
+
+    begun = 0
+
+    def send_columns(count):
+        nonlocal begun
+        for copy in wo_copies[begun:begun + count]:
+            copy.start()
+        begun += count
 
     raw = None
     for n in range(KPARTS):
         with scope("load%d" % n):
             pltpu.make_async_copy(both_parts, both_parts, load_sem.at[n]).wait()
-        if n == 0:
-            w_kept = load(late, w_hbm.at[1 + kept], w.at[:, pl.ds(cols, cols)])
-        if n == 1:
-            small = [
-                load(late + 1, decay_hbm, decay), load(late + 2, frames_hbm, frames),
-                load(late + 3, opened_hbm, opened),
-            ]
-            x_head = load(late + 4, x_hbm.at[pl.ds(0, top)], x.at[pl.ds(0, top)])
         if n == KPARTS - 1:
             with scope("bar"):
                 pl.semaphore_wait(barrier, n_mp + 1 + (c + n_span - 1) // n_span - (c + 1) // n_span)
-            for copy in wo_copies:
-                copy.start()
-        at = slice(n * deep, (n + 1) * deep)
+            send_columns(2 * (chips - 1))
         with scope("sent%d" % n):
-            step = jnp.dot(x[top:, at], w[at, :HD], preferred_element_type=jnp.float32)
-            raw = step if raw is None else raw + step
+            for start in range(n * deep, (n + 1) * deep, deep // 2):
+                at = slice(start, start + deep // 2)
+                step = jnp.dot(x[top:, at], w[at, :HD], preferred_element_type=jnp.float32)
+                raw = step if raw is None else raw + step
     with scope("unit"):
         keep(raw, top, MEM, 0, 0)
     send_tail(0)
     wo_side.start()
-    w_query = load(late + 5, w_hbm.at[0], w.at[:, pl.ds(2 * cols, cols)])
-    wo_own = load(late + 6, wo_hbm.at[:, columns_of(me)], wo.at[me])
-    with scope("sentrest"):
-        raw = project(top, MEM, HD, cols - HD)
-        for i in range(1, heads):
-            keep(raw, top, MEM, i, i - 1)
-    with scope("loadk"):
-        w_kept.wait()
-    with scope("kept"):
-        raw = project(top, MEM, cols, cols)
-        for i in range(heads):
-            keep(raw, top, MEM, heads + i, i)
-    with scope("loadh"):
-        x_head.wait()
-
-    def head_rows(pair):
-        with scope("headkv"):
-            raw = project(0, top, pair * HD, 2 * HD)
-            for at in range(2):
-                keep(raw, 0, top, pair + at, at)
-
     for copy in small:
         copy.wait()
+    wide = -(-(3 * heads - 1) // 2)
+    with scope("loadk"):
+        w_sent.wait()
+        w_kept.wait()
+    with scope("tail1"):
+        columns(top, MEM, 1, 1 + wide)
+    send_tail(1)
+    send_columns(chips - 1)
+    with scope("loadq"):
+        w_query.wait()
+    with scope("tail2"):
+        columns(top, MEM, 1 + wide, 3 * heads)
+    for i in range(2, heads):
+        send_tail(i)
+    with scope("loadx"):
+        x_head.wait()
     halo_from = pl.multiple_of(HALF + other * (rows - HALF), HALF)
     halo = remote(
         kv.at[:, :, pl.ds(halo_from, HALF)], kv.at[:, :, pl.ds(blank, HALF)],
@@ -274,14 +286,12 @@
 
             later = r0 * state + low
             m_out[i, rows_at, :] = jnp.where(is0, later, state).astype(jnp.bfloat16)
-            moved_copy(k, i, r).start()
+
+            @pl.when(c > 0)
+            def _():
+                moved_copy(k, i, r).start()
+
             mem[kept, i, rows_at, :] = jnp.where(is0, state, later).astype(jnp.bfloat16)
-
-    def queries(first, count):
-        with scope("queries"):
-            raw = project(first, count, 2 * cols, cols)
-            for i in range(heads):
-                q[i, HALF + first:HALF + first + count, :] = unit(raw[:, i * HD:(i + 1) * HD], None)
 
     def frame_rows():
         total = frames.shape[1]
@@ -399,39 +409,47 @@
             with scope("chain%d" % place):
                 chain_head(i)
 
-    for pair in range(0, 2 * heads, 2):
-        head_rows(pair)
-        if pair == 0:
-            send_tail(1)
+    chain_at(0)
+    with scope("head1"):
+        columns(0, top, 0, wide)
+    send_columns(chips - 1)
+    with scope("head2"):
+        columns(0, top, wide, 2 * wide)
     halo.start()
-    chain_at(0)
-    with scope("loadq"):
-        w_query.wait()
-    queries(0, top)
-    for i in range(2, heads):
-        send_tail(i)
+    chain_at(1)
+    with scope("head3"):
+        columns(0, top, 2 * wide, 3 * heads)
+    send_columns(chips - 1)
+    chain_at(2)
     relay_head(0, 0)
-    queries(top, rows - top)
-    chain_at(1)
-    relay_head(0, 1)
+    relay_up(0, acrosses[0])
     with scope("local"):
         frame_rows()
         for g in range(1, groups - 1):
             local_group(g)
+    send_columns(len(wo_copies))
+    chain_at(3)
+
+    @pl.when(c == 0)
+    def _():
+        for copy in each(moved_copy):
+            copy.start()
+
+    relay_head(0, 1)
+    chain_at(4)
+    with scope("local"):
         with scope("halo"):
             halo.wait_recv()
         local_group(0)
         local_group(groups - 1)
-    chain_at(2)
     relay_head(1, 0)
-    chain_at(3)
+    chain_at(5)
     relay_head(1, 1)
-    chain_at(4)
+    chain_at(6)
     relay_head(2, 0)
     memory_head(0)
-    chain_at(5)
+    chain_at(7)
     relay_up(per_head, 2 * per_head + per_head // 2)
-    chain_at(6)
     relay_head(2, 1)
     memory_head(1)
     relay_up(2 * per_head + per_head // 2, heads * per_head)
@@ -472,30 +490,34 @@
             at = slice(first, first + 2 * GROUP)
             acc[at, :] = x[at, own].astype(jnp.float32) + product([me], range(heads), first, 2 * GROUP)
     early = range(heads - 1)
-    for i in early:
-        for j in order[i]:
-            cross(j)
+    for j in order[0]:
+        cross(j)
     with scope("waitside"):
         wo_side.wait_recv()
         remote(att.at[me], att.at[me], a_send, a_recv, {"mp": sib}).wait_recv()
     add([sib], range(heads), "near")
+    for i in early[1:]:
+        for j in order[i]:
+            cross(j)
     for i in early:
         far_weights(i)
     add(far[0::2], early, "direct")
     final = order[heads - 1]
-    for j in final[:2]:
+    for j in final[:-1]:
         cross(j)
     arrived(att.at[pl.ds(0, chips - 1), pl.ds(0, heads - 1)], 0)
     add(far[1::2], early, "passed")
     far_weights(heads - 1)
+    cross(final[-1])
     for n, j in enumerate(final):
-        if n + 2 < len(final):
-            cross(final[n + 2])
         first, count = spots[j][1], spots[j][2]
         arrived(att.at[pl.ds(0, chips - 1), heads - 1, pl.ds(first, count)], 1 + n)
-        with scope("fin"):
-            at = slice(first, first + count)
-            out[at, :] = (acc[at, :] + product(far, [heads - 1], first, count)).astype(jnp.bfloat16)
+        if n % 2:
+            with scope("fin"):
+                at = slice(first - count, first + count)
+                out[at, :] = (
+                    acc[at, :] + product(far, [heads - 1], first - count, 2 * count)
+                ).astype(jnp.bfloat16)
 
     with scope("sends"):
         tail_all = kv.at[sent, :, pl.ds(tail0, MEM)]
@@ -523,12 +545,12 @@
 
         @pl.when(c == last - 1)
         def _():
-            lot = wo.at[pl.ds(0, chips - 1), pl.ds(0, (heads - 1) * HD)]
+            lot = wo.at[pl.ds(0, chips - 1), pl.ds(0, cols - block)]
             remote(lot, lot, wu_send, wr_recv.at[0], {"phase": other}).wait_send()
 
         @pl.when(c == last)
         def _():
-            lot = wo.at[pl.ds(0, chips - 1), pl.ds(0, HD)]
+            lot = wo.at[pl.ds(0, chips - 1), pl.ds(0, block)]
             remote(lot, lot, wu_send, wr_recv.at[0], {"phase": other}).wait_send()
 
 
@@ -575,7 +597,7 @@
             pltpu.VMEM((heads, MEM, HD), bf16),
             pltpu.VMEM((heads, MEM, HD), bf16),
             pltpu.VMEM((2, heads, MEM, HD), bf16),
-            dma((KPARTS + 7,)),
+            dma((KPARTS + 8,)),
             dma, dma,
             dma, dma((chunks,)), dma, dma, dma((heads,)),
             dma, dma((pieces,)),

time: 31.2 us -> 29.5 us (0.946)
  Pallas kernels: 30.2 us -> 28.5 us
    pallas_call x1, Pallas kernels: 30.2 us -> 28.5 us  [local(): pl.pallas_call(functools.partial(body, (n_span, n_mp, rows, width, cols))...]
where the time goes in v3:
time: 29.5 us; the launch traced here: 29.3 us
  Pallas kernels  28.5 us (97%)
  local copies, waits for them, and re-layouts  0.84 us (3%)
    pallas_call x1, Pallas kernels, local(): pl.pallas_call(functools.partial(body, (n_span, n_mp, rows, width, cols))...  28.5 us
    unnamed x1, local copies, waits for them, and re-layouts  0.84 us

profile of v3, /device:TPU:25, one launch (start us, length us, event | category | flops | bytes accessed | tf_op | source)
XLA Modules:
  0.0 29.3 jit_solution(5074700560938946855)
XLA Ops:
  0.0 28.5 %refiner.1 = bf16[512,640]{1,0:T(8,128)(2,1)S(1)} custom-call(bf16[512,2560]{1,0:T(8,128)(2,1)} %x_hbm.1, bf16[3,2560,384]{2,1,0:T(8,128)(2,1)} %bitcast.2, bf16[384,2560]{1,0:T(8,128)(2,1)} %wo_hbm.1, f32[2,3]{1,0:T(2,128)} %bitcast.3, s32[1,1024]{1,0:T(1,128)} %frames_hbm.1, s32[1,17]{1,0:T(1,128)} %opened_hbm.1), custom_call_target="tpu_custom_call" | custom-call | flops 4026531840 | bytes 12582912 | tf_op jit(solution)/shard_map/refiner/pallas_call | solution.py:576
  28.5 0.8 %copy.8 = bf16[512,640]{1,0:T(8,128)(2,1)} copy(bf16[512,640]{1,0:T(8,128)(2,1)S(1)} %refiner.1) | data formatting | bytes 1310720

commit v4 on v3

--- a/solution.py
+++ b/solution.py
@@ -15,8 +15,9 @@
 HALF = WIN // 2
 GROUP = 128
 CUTS = 4
+DIRECT = 2
 KPARTS = 2
-PLAN = ((0, 1, 3), (2, 4, 5), (4, 5, 6), (5, 6, 7))
+PLAN = ((0, 1, 3), (2, 4, 5), (4, 5, 7), (4, 6, 7))
 MESH = pl.DeviceIdType.MESH
 
 outside_frame = 1048576
@@ -346,6 +347,16 @@
         crosses.append(across)
         relays.append(passed)
 
+    direct = {}
+    for n, j in enumerate(range(len(spots) - DIRECT, len(spots))):
+        i, first, count = spots[j]
+        mine = att.at[me, i, pl.ds(first, count)]
+        direct[j] = [
+            remote(mine, mine, r_send, r_recv.at[1 + rows // GROUP - DIRECT + n], {"mp": (sib + 2 * o) % n_mp})
+            for o in range(1, chips)
+        ]
+    even = me % 2 == 0
+
     start = phase * (rows // WIN)
 
     def memory_groups(i, members):
@@ -386,6 +397,11 @@
                     if which == i and base <= first < base + 2 * GROUP:
                         for copy in crosses[j]:
                             copy.start()
+                        if j in direct:
+                            @pl.when(even)
+                            def _(copies=direct[j]):
+                                for copy in copies:
+                                    copy.start()
                         sides[j].start()
 
     def relay_head(i, n):
@@ -413,14 +429,20 @@
     with scope("head1"):
         columns(0, top, 0, wide)
     send_columns(chips - 1)
+    chain_at(1)
     with scope("head2"):
         columns(0, top, wide, 2 * wide)
     halo.start()
-    chain_at(1)
+
+    @pl.when(c == 0)
+    def _():
+        for r in range(CUTS):
+            moved_copy(r, 0, r).start()
+
+    chain_at(2)
     with scope("head3"):
         columns(0, top, 2 * wide, 3 * heads)
     send_columns(chips - 1)
-    chain_at(2)
     relay_head(0, 0)
     relay_up(0, acrosses[0])
     with scope("local"):
@@ -432,8 +454,9 @@
 
     @pl.when(c == 0)
     def _():
-        for copy in each(moved_copy):
-            copy.start()
+        for i in range(1, heads):
+            for r in range(CUTS):
+                moved_copy(i * CUTS + r, i, r).start()
 
     relay_head(0, 1)
     chain_at(4)
@@ -446,9 +469,9 @@
     chain_at(5)
     relay_head(1, 1)
     chain_at(6)
-    relay_head(2, 0)
     memory_head(0)
     chain_at(7)
+    relay_head(2, 0)
     relay_up(per_head, 2 * per_head + per_head // 2)
     relay_head(2, 1)
     memory_head(1)
@@ -472,7 +495,12 @@
         for o in range(chips - 1):
             with scope("waitcross"):
                 crosses[j][o].wait_recv()
-            relays[j][o].start()
+            if j in direct:
+                @pl.when(jnp.logical_not(even))
+                def _(copy=relays[j][o]):
+                    copy.start()
+            else:
+                relays[j][o].start()
 
     def arrived(lot, which):
         with scope("waitrelay"):
@@ -503,12 +531,11 @@
         far_weights(i)
     add(far[0::2], early, "direct")
     final = order[heads - 1]
-    for j in final[:-1]:
+    for j in final:
         cross(j)
     arrived(att.at[pl.ds(0, chips - 1), pl.ds(0, heads - 1)], 0)
     add(far[1::2], early, "passed")
     far_weights(heads - 1)
-    cross(final[-1])
     for n, j in enumerate(final):
         first, count = spots[j][1], spots[j][2]
         arrived(att.at[pl.ds(0, chips - 1), heads - 1, pl.ds(first, count)], 1 + n)

time: 29.5 us -> 28.7 us (0.973)
  Pallas kernels: 28.5 us -> 27.6 us
    pallas_call x1, Pallas kernels: 28.5 us -> 27.6 us  [local(): pl.pallas_call(functools.partial(body, (n_span, n_mp, rows, width, cols))...]
where the time goes in v4:
time: 28.7 us; the launch traced here: 28.5 us
  Pallas kernels  27.6 us (96%)
  local copies, waits for them, and re-layouts  0.84 us (3%)
    pallas_call x1, Pallas kernels, local(): pl.pallas_call(functools.partial(body, (n_span, n_mp, rows, width, cols))...  27.6 us
    unnamed x1, local copies, waits for them, and re-layouts  0.84 us

profile of v4, /device:TPU:25, one launch (start us, length us, event | category | flops | bytes accessed | tf_op | source)
XLA Modules:
  0.0 28.5 jit_solution(8565993860856464987)
XLA Ops:
  0.0 27.6 %refiner.1 = bf16[512,640]{1,0:T(8,128)(2,1)S(1)} custom-call(bf16[512,2560]{1,0:T(8,128)(2,1)} %x_hbm.1, bf16[3,2560,384]{2,1,0:T(8,128)(2,1)} %bitcast.2, bf16[384,2560]{1,0:T(8,128)(2,1)} %wo_hbm.1, f32[2,3]{1,0:T(2,128)} %bitcast.3, s32[1,1024]{1,0:T(1,128)} %frames_hbm.1, s32[1,17]{1,0:T(1,128)} %opened_hbm.1), custom_call_target="tpu_custom_call" | custom-call | flops 4026531840 | bytes 12582912 | tf_op jit(solution)/shard_map/refiner/pallas_call | solution.py:603
  27.6 0.8 %copy.8 = bf16[512,640]{1,0:T(8,128)(2,1)} copy(bf16[512,640]{1,0:T(8,128)(2,1)S(1)} %refiner.1) | data formatting | bytes 1310720

commit v5 on v4

--- a/solution.py
+++ b/solution.py
@@ -16,8 +16,8 @@
 GROUP = 128
 CUTS = 4
 DIRECT = 2
-KPARTS = 2
-PLAN = ((0, 1, 3), (2, 4, 5), (4, 5, 7), (4, 6, 7))
+ROW_PARTS = 2
+PLAN = ((0, 1, 2), (2, 3, 5), (4, 5, 7), (4, 6, 7))
 MESH = pl.DeviceIdType.MESH
 
 outside_frame = 1048576
@@ -60,6 +60,29 @@
     piece = MEM // CUTS
     last = n_span - 1
 
+    def load(i, src, dst):
+        copy = pltpu.make_async_copy(src, dst, load_sem.at[i])
+        copy.start()
+        return copy
+
+    deep = width // 2
+    rows_part = MEM // ROW_PARTS
+    x_tails = []
+    for n in range(ROW_PARTS):
+        at = pl.ds(top + n * rows_part, rows_part)
+        x_tails.append(load(n, x_hbm.at[at], x.at[at]))
+        if n == 0:
+            load(n, w_hbm.at[1 + sent, :, pl.ds(0, HD)], w.at[:, pl.ds(0, HD)])
+    first_loads = w.at[:, pl.ds(0, rows_part + HD)]
+    w_sent = load(ROW_PARTS, w_hbm.at[1 + sent, :, pl.ds(HD, cols - HD)], w.at[:, pl.ds(HD, cols - HD)])
+    w_kept = load(ROW_PARTS + 1, w_hbm.at[1 + kept], w.at[:, pl.ds(cols, cols)])
+    w_query = load(ROW_PARTS + 2, w_hbm.at[0], w.at[:, pl.ds(2 * cols, cols)])
+    small = [
+        load(ROW_PARTS + 3, decay_hbm, decay), load(ROW_PARTS + 4, frames_hbm, frames), load(ROW_PARTS + 5, opened_hbm, opened),
+    ]
+    x_head = load(ROW_PARTS + 6, x_hbm.at[pl.ds(0, top)], x.at[pl.ds(0, top)])
+    wo_own = load(ROW_PARTS + 7, wo_hbm.at[:, pl.ds(pl.multiple_of(me * share, HD), share)], wo.at[me])
+
     barrier = pltpu.get_barrier_semaphore()
     for o in range(1, n_mp):
         pl.semaphore_signal(barrier, inc=1, device_id={"mp": (me + o) % n_mp}, device_id_type=MESH)
@@ -72,26 +95,6 @@
     @pl.when(c < last)
     def _():
         pl.semaphore_signal(barrier, inc=1, device_id={"span": c + 1}, device_id_type=MESH)
-
-    def load(i, src, dst):
-        copy = pltpu.make_async_copy(src, dst, load_sem.at[i])
-        copy.start()
-        return copy
-
-    deep = width // KPARTS
-    for n in range(KPARTS):
-        at = pl.ds(n * deep, deep)
-        load(n, x_hbm.at[pl.ds(top, MEM), at], x.at[pl.ds(top, MEM), at])
-        load(n, w_hbm.at[1 + sent, at, pl.ds(0, HD)], w.at[at, pl.ds(0, HD)])
-    both_parts = w.at[pl.ds(0, deep), pl.ds(0, MEM + HD)]
-    w_sent = load(KPARTS, w_hbm.at[1 + sent, :, pl.ds(HD, cols - HD)], w.at[:, pl.ds(HD, cols - HD)])
-    w_kept = load(KPARTS + 1, w_hbm.at[1 + kept], w.at[:, pl.ds(cols, cols)])
-    w_query = load(KPARTS + 2, w_hbm.at[0], w.at[:, pl.ds(2 * cols, cols)])
-    small = [
-        load(KPARTS + 3, decay_hbm, decay), load(KPARTS + 4, frames_hbm, frames), load(KPARTS + 5, opened_hbm, opened),
-    ]
-    x_head = load(KPARTS + 6, x_hbm.at[pl.ds(0, top)], x.at[pl.ds(0, top)])
-    wo_own = load(KPARTS + 7, wo_hbm.at[:, pl.ds(pl.multiple_of(me * share, HD), share)], wo.at[me])
 
     zero_rows = kv.shape[2] - (HALF + rows + HALF)
     kv[:, :, HALF + rows + HALF:, :] = jnp.zeros((2, heads, zero_rows, HD), jnp.bfloat16)
@@ -134,18 +137,17 @@
     wo_side = remote(wo_hbm.at[:, columns_of(sib)], wo.at[me], ws_send, ws_recv, {"mp": sib})
     per_head = len(far)
 
+    lazy = (c == 0) & (n_span > 2)
+
     def relay(at):
-        with scope("relay"):
-            wo_copies[at].wait_recv()
+        @pl.when(jnp.logical_not(lazy))
+        def _():
+            with scope("relay"):
+                wo_copies[at].wait_recv()
 
         @pl.when(c > 0)
         def _():
             wo_downs[at].start()
-
-        if at in acrosses:
-            @pl.when(c == last)
-            def _():
-                wo_acrosses[at - acrosses[0]].start()
 
     def relay_up(first, end):
         @pl.when(c == last - 1)
@@ -210,22 +212,27 @@
             copy.start()
         begun += count
 
-    raw = None
-    for n in range(KPARTS):
+    for n in range(ROW_PARTS):
         with scope("load%d" % n):
-            pltpu.make_async_copy(both_parts, both_parts, load_sem.at[n]).wait()
-        if n == KPARTS - 1:
+            if n == 0:
+                pltpu.make_async_copy(first_loads, first_loads, load_sem.at[n]).wait()
+            else:
+                x_tails[n].wait()
+        first = top + n * rows_part
+        with scope("sent%d" % n):
+            raw = jnp.dot(
+                x[first:first + rows_part, :deep], w[:deep, :HD], preferred_element_type=jnp.float32
+            ) + jnp.dot(
+                x[first:first + rows_part, deep:], w[deep:, :HD], preferred_element_type=jnp.float32
+            )
+            keep(raw, first, rows_part, 0, 0)
+        if n == 0:
             with scope("bar"):
                 pl.semaphore_wait(barrier, n_mp + 1 + (c + n_span - 1) // n_span - (c + 1) // n_span)
+        for r in range(n * CUTS // ROW_PARTS, (n + 1) * CUTS // ROW_PARTS):
+            tails[r].start()
+        if n == 0:
             send_columns(2 * (chips - 1))
-        with scope("sent%d" % n):
-            for start in range(n * deep, (n + 1) * deep, deep // 2):
-                at = slice(start, start + deep // 2)
-                step = jnp.dot(x[top:, at], w[at, :HD], preferred_element_type=jnp.float32)
-                raw = step if raw is None else raw + step
-    with scope("unit"):
-        keep(raw, top, MEM, 0, 0)
-    send_tail(0)
     wo_side.start()
     for copy in small:
         copy.wait()
@@ -430,34 +437,35 @@
         columns(0, top, 0, wide)
     send_columns(chips - 1)
     chain_at(1)
+
+    @pl.when(c == 0)
+    def _():
+        for r in range(CUTS):
+            moved_copy(r, 0, r).start()
+
     with scope("head2"):
         columns(0, top, wide, 2 * wide)
     halo.start()
 
+    chain_at(2)
+
     @pl.when(c == 0)
     def _():
-        for r in range(CUTS):
-            moved_copy(r, 0, r).start()
-
-    chain_at(2)
+        for i in range(1, heads):
+            for r in range(CUTS):
+                moved_copy(i * CUTS + r, i, r).start()
+
     with scope("head3"):
         columns(0, top, 2 * wide, 3 * heads)
     send_columns(chips - 1)
     relay_head(0, 0)
     relay_up(0, acrosses[0])
+    chain_at(3)
     with scope("local"):
         frame_rows()
         for g in range(1, groups - 1):
             local_group(g)
     send_columns(len(wo_copies))
-    chain_at(3)
-
-    @pl.when(c == 0)
-    def _():
-        for i in range(1, heads):
-            for r in range(CUTS):
-                moved_copy(i * CUTS + r, i, r).start()
-
     relay_head(0, 1)
     chain_at(4)
     with scope("local"):
@@ -472,10 +480,15 @@
     memory_head(0)
     chain_at(7)
     relay_head(2, 0)
-    relay_up(per_head, 2 * per_head + per_head // 2)
+    memory_head(1)
     relay_head(2, 1)
-    memory_head(1)
-    relay_up(2 * per_head + per_head // 2, heads * per_head)
+    relay_up(per_head, heads * per_head)
+
+    @pl.when(c == last)
+    def _():
+        for copy in wo_acrosses:
+            copy.start()
+
     memory_head(2)
 
     own = pl.ds(pl.multiple_of(me * share, HD), share)
@@ -510,6 +523,12 @@
         with scope("waitwo"):
             lot = wo.at[pl.ds(0, chips - 1), pl.ds(0, HD)]
             remote(lot, lot, wd_send, wr_recv.at[i], {"phase": other}).wait_recv()
+
+            @pl.when(lazy)
+            def _():
+                for at in range(i * per_head, (i + 1) * per_head):
+                    wo_copies[at].wait_recv()
+
 
     order = [[j for j, spot in enumerate(spots) if spot[0] == i] for i in range(heads)]
     wo_own.wait()
@@ -531,20 +550,39 @@
         far_weights(i)
     add(far[0::2], early, "direct")
     final = order[heads - 1]
-    for j in final:
+    half = len(final) // 2
+
+    def passed():
+        arrived(att.at[pl.ds(0, chips - 1), pl.ds(0, heads - 1)], 0)
+        add(far[1::2], early, "passed")
+        far_weights(heads - 1)
+
+    def finish(n):
+        first, count = spots[final[n]][1], half * spots[final[n]][2]
+        for k in range(n, n + half):
+            piece_at = pl.ds(spots[final[k]][1], spots[final[k]][2])
+            arrived(att.at[pl.ds(0, chips - 1), heads - 1, piece_at], 1 + k)
+        with scope("fin"):
+            at = slice(first, first + count)
+            out[at, :] = (acc[at, :] + product(far, [heads - 1], first, count)).astype(jnp.bfloat16)
+
+    for j in final[:half]:
         cross(j)
-    arrived(att.at[pl.ds(0, chips - 1), pl.ds(0, heads - 1)], 0)
-    add(far[1::2], early, "passed")
-    far_weights(heads - 1)
-    for n, j in enumerate(final):
-        first, count = spots[j][1], spots[j][2]
-        arrived(att.at[pl.ds(0, chips - 1), heads - 1, pl.ds(first, count)], 1 + n)
-        if n % 2:
-            with scope("fin"):
-                at = slice(first - count, first + count)
-                out[at, :] = (
-                    acc[at, :] + product(far, [heads - 1], first - count, 2 * count)
-                ).astype(jnp.bfloat16)
+
+    @pl.when(even)
+    def _():
+        passed()
+        finish(0)
+
+    for j in final[half:]:
+        cross(j)
+
+    @pl.when(jnp.logical_not(even))
+    def _():
+        passed()
+        finish(0)
+
+    finish(half)
 
     with scope("sends"):
         tail_all = kv.at[sent, :, pl.ds(tail0, MEM)]
@@ -624,7 +662,7 @@
             pltpu.VMEM((heads, MEM, HD), bf16),
             pltpu.VMEM((heads, MEM, HD), bf16),
             pltpu.VMEM((2, heads, MEM, HD), bf16),
-            dma((KPARTS + 8,)),
+            dma((ROW_PARTS + 8,)),
             dma, dma,
             dma, dma((chunks,)), dma, dma, dma((heads,)),
             dma, dma((pieces,)),

time: 28.7 us -> 28.3 us (0.986)
  Pallas kernels: 27.6 us -> 27.3 us
    pallas_call x1, Pallas kernels: 27.6 us -> 27.3 us  [local(): pl.pallas_call(functools.partial(body, (n_span, n_mp, rows, width, cols))...]
where the time goes in v5:
time: 28.3 us; the launch traced here: 28.2 us
  Pallas kernels  27.3 us (96%)
  local copies, waits for them, and re-layouts  0.84 us (3%)
    pallas_call x1, Pallas kernels, local(): pl.pallas_call(functools.partial(body, (n_span, n_mp, rows, width, cols))...  27.3 us
    unnamed x1, local copies, waits for them, and re-layouts  0.84 us

profile of v5, /device:TPU:25, one launch (start us, length us, event | category | flops | bytes accessed | tf_op | source)
XLA Modules:
  0.0 28.2 jit_solution(11598211165590951425)
XLA Ops:
  0.0 27.3 %refiner.1 = bf16[512,640]{1,0:T(8,128)(2,1)S(1)} custom-call(bf16[512,2560]{1,0:T(8,128)(2,1)} %x_hbm.1, bf16[3,2560,384]{2,1,0:T(8,128)(2,1)} %bitcast.2, bf16[384,2560]{1,0:T(8,128)(2,1)} %wo_hbm.1, f32[2,3]{1,0:T(2,128)} %bitcast.3, s32[1,1024]{1,0:T(1,128)} %frames_hbm.1, s32[1,17]{1,0:T(1,128)} %opened_hbm.1), custom_call_target="tpu_custom_call" | custom-call | flops 4026531840 | bytes 12582912 | tf_op jit(solution)/shard_map/refiner/pallas_call | solution.py:641
  27.4 0.8 %copy.8 = bf16[512,640]{1,0:T(8,128)(2,1)} copy(bf16[512,640]{1,0:T(8,128)(2,1)S(1)} %refiner.1) | data formatting | bytes 1310720

commit v6 on v5

--- a/solution.py
+++ b/solution.py
@@ -17,7 +17,7 @@
 CUTS = 4
 DIRECT = 2
 ROW_PARTS = 2
-PLAN = ((0, 1, 2), (2, 3, 5), (4, 5, 7), (4, 6, 7))
+PLAN = ((0, 1, 2), (2, 3, 5), (4, 8, 7), (4, 6, 7))
 MESH = pl.DeviceIdType.MESH
 
 outside_frame = 1048576
@@ -74,14 +74,14 @@
         if n == 0:
             load(n, w_hbm.at[1 + sent, :, pl.ds(0, HD)], w.at[:, pl.ds(0, HD)])
     first_loads = w.at[:, pl.ds(0, rows_part + HD)]
-    w_sent = load(ROW_PARTS, w_hbm.at[1 + sent, :, pl.ds(HD, cols - HD)], w.at[:, pl.ds(HD, cols - HD)])
-    w_kept = load(ROW_PARTS + 1, w_hbm.at[1 + kept], w.at[:, pl.ds(cols, cols)])
-    w_query = load(ROW_PARTS + 2, w_hbm.at[0], w.at[:, pl.ds(2 * cols, cols)])
+    load(ROW_PARTS, w_hbm.at[1 + sent, :, pl.ds(HD, cols - HD)], w.at[:, pl.ds(HD, cols - HD)])
+    load(ROW_PARTS, w_hbm.at[1 + kept], w.at[:, pl.ds(cols, cols)])
+    w_query = load(ROW_PARTS + 1, w_hbm.at[0], w.at[:, pl.ds(2 * cols, cols)])
     small = [
-        load(ROW_PARTS + 3, decay_hbm, decay), load(ROW_PARTS + 4, frames_hbm, frames), load(ROW_PARTS + 5, opened_hbm, opened),
+        load(ROW_PARTS + 2, decay_hbm, decay), load(ROW_PARTS + 3, frames_hbm, frames), load(ROW_PARTS + 4, opened_hbm, opened),
     ]
-    x_head = load(ROW_PARTS + 6, x_hbm.at[pl.ds(0, top)], x.at[pl.ds(0, top)])
-    wo_own = load(ROW_PARTS + 7, wo_hbm.at[:, pl.ds(pl.multiple_of(me * share, HD), share)], wo.at[me])
+    x_head = load(ROW_PARTS + 5, x_hbm.at[pl.ds(0, top)], x.at[pl.ds(0, top)])
+    wo_own = load(ROW_PARTS + 6, wo_hbm.at[:, pl.ds(pl.multiple_of(me * share, HD), share)], wo.at[me])
 
     barrier = pltpu.get_barrier_semaphore()
     for o in range(1, n_mp):
@@ -238,8 +238,8 @@
         copy.wait()
     wide = -(-(3 * heads - 1) // 2)
     with scope("loadk"):
-        w_sent.wait()
-        w_kept.wait()
+        both = w.at[:, pl.ds(HD, 2 * cols - HD)]
+        pltpu.make_async_copy(both, both, load_sem.at[ROW_PARTS]).wait()
     with scope("tail1"):
         columns(top, MEM, 1, 1 + wide)
     send_tail(1)
@@ -435,7 +435,7 @@
     chain_at(0)
     with scope("head1"):
         columns(0, top, 0, wide)
-    send_columns(chips - 1)
+    send_columns(len(wo_copies))
     chain_at(1)
 
     @pl.when(c == 0)
@@ -457,7 +457,6 @@
 
     with scope("head3"):
         columns(0, top, 2 * wide, 3 * heads)
-    send_columns(chips - 1)
     relay_head(0, 0)
     relay_up(0, acrosses[0])
     chain_at(3)
@@ -465,9 +464,9 @@
         frame_rows()
         for g in range(1, groups - 1):
             local_group(g)
-    send_columns(len(wo_copies))
     relay_head(0, 1)
     chain_at(4)
+    chain_at(8)
     with scope("local"):
         with scope("halo"):
             halo.wait_recv()
@@ -557,9 +556,9 @@
         add(far[1::2], early, "passed")
         far_weights(heads - 1)
 
-    def finish(n):
-        first, count = spots[final[n]][1], half * spots[final[n]][2]
-        for k in range(n, n + half):
+    def finish(n, size):
+        first, count = spots[final[n]][1], size * spots[final[n]][2]
+        for k in range(n, n + size):
             piece_at = pl.ds(spots[final[k]][1], spots[final[k]][2])
             arrived(att.at[pl.ds(0, chips - 1), heads - 1, piece_at], 1 + k)
         with scope("fin"):
@@ -572,17 +571,19 @@
     @pl.when(even)
     def _():
         passed()
-        finish(0)
+        finish(0, half)
 
     for j in final[half:]:
         cross(j)
 
+    @pl.when(even)
+    def _():
+        finish(half, len(final) - half)
+
     @pl.when(jnp.logical_not(even))
     def _():
         passed()
-        finish(0)
-
-    finish(half)
+        finish(0, len(final))
 
     with scope("sends"):
         tail_all = kv.at[sent, :, pl.ds(tail0, MEM)]
@@ -662,7 +663,7 @@
             pltpu.VMEM((heads, MEM, HD), bf16),
             pltpu.VMEM((heads, MEM, HD), bf16),
             pltpu.VMEM((2, heads, MEM, HD), bf16),
-            dma((ROW_PARTS + 8,)),
+            dma((ROW_PARTS + 7,)),
             dma, dma,
             dma, dma((chunks,)), dma, dma, dma((heads,)),
             dma, dma((pieces,)),

time: 28.3 us -> 28.1 us (level)
  no operation moved by 1% of the time
where the time goes in v6:
time: 28.1 us; the launch traced here: 27.9 us
  Pallas kernels  27.1 us (96%)
  local copies, waits for them, and re-layouts  0.84 us (3%)
    pallas_call x1, Pallas kernels, local(): pl.pallas_call(functools.partial(body, (n_span, n_mp, rows, width, cols))...  27.1 us
    unnamed x1, local copies, waits for them, and re-layouts  0.84 us

profile of v6, /device:TPU:25, one launch (start us, length us, event | category | flops | bytes accessed | tf_op | source)
XLA Modules:
  0.0 27.9 jit_solution(10029644267656709491)
XLA Ops:
  0.0 27.1 %refiner.1 = bf16[512,640]{1,0:T(8,128)(2,1)S(1)} custom-call(bf16[512,2560]{1,0:T(8,128)(2,1)} %x_hbm.1, bf16[3,2560,384]{2,1,0:T(8,128)(2,1)} %bitcast.2, bf16[384,2560]{1,0:T(8,128)(2,1)} %wo_hbm.1, f32[2,3]{1,0:T(2,128)} %bitcast.3, s32[1,1024]{1,0:T(1,128)} %frames_hbm.1, s32[1,17]{1,0:T(1,128)} %opened_hbm.1), custom_call_target="tpu_custom_call" | custom-call | flops 4026531840 | bytes 12582912 | tf_op jit(solution)/shard_map/refiner/pallas_call | solution.py:642
  27.1 0.8 %copy.8 = bf16[512,640]{1,0:T(8,128)(2,1)} copy(bf16[512,640]{1,0:T(8,128)(2,1)S(1)} %refiner.1) | data formatting | bytes 1310720

commit v7 on v6

--- a/solution.py
+++ b/solution.py
@@ -17,7 +17,7 @@
 CUTS = 4
 DIRECT = 2
 ROW_PARTS = 2
-PLAN = ((0, 1, 2), (2, 3, 5), (4, 8, 7), (4, 6, 7))
+PLAN = ((0, 1, 2), (2, 3, 4), (4, 8, 6), (4, 5, 7))
 MESH = pl.DeviceIdType.MESH
 
 outside_frame = 1048576
@@ -422,6 +422,8 @@
             plan.setdefault(place, []).append((kind, i))
 
     def chain_at(place):
+        if place not in plan:
+            return
         kind, i = jnp.minimum(c, len(PLAN) - 1), jnp.int32(heads)
         for which, head in plan[place]:
             if head < heads:

time: 28.1 us -> 28 us (level)
  no operation moved by 1% of the time
where the time goes in v7:
time: 28 us; the launch traced here: 27.8 us
  Pallas kernels  27 us (96%)
  local copies, waits for them, and re-layouts  0.84 us (3%)
    pallas_call x1, Pallas kernels, local(): pl.pallas_call(functools.partial(body, (n_span, n_mp, rows, width, cols))...  27 us
    unnamed x1, local copies, waits for them, and re-layouts  0.84 us

profile of v7, /device:TPU:25, one launch (start us, length us, event | category | flops | bytes accessed | tf_op | source)
XLA Modules:
  0.0 27.8 jit_solution(2867697021149699641)
XLA Ops:
  0.0 27.0 %refiner.1 = bf16[512,640]{1,0:T(8,128)(2,1)S(1)} custom-call(bf16[512,2560]{1,0:T(8,128)(2,1)} %x_hbm.1, bf16[3,2560,384]{2,1,0:T(8,128)(2,1)} %bitcast.2, bf16[384,2560]{1,0:T(8,128)(2,1)} %wo_hbm.1, f32[2,3]{1,0:T(2,128)} %bitcast.3, s32[1,1024]{1,0:T(1,128)} %frames_hbm.1, s32[1,17]{1,0:T(1,128)} %opened_hbm.1), custom_call_target="tpu_custom_call" | custom-call | flops 4026531840 | bytes 12582912 | tf_op jit(solution)/shard_map/refiner/pallas_call | solution.py:644
  27.0 0.8 %copy.8 = bf16[512,640]{1,0:T(8,128)(2,1)} copy(bf16[512,640]{1,0:T(8,128)(2,1)S(1)} %refiner.1) | data formatting | bytes 1310720
